TPU v7x, 32 devices: a whole 2x2x4 slice. The times are simulated.
32 devices in a mesh: lat: 4 (over x, core), lev: 8 (over z, y).
Axes of the slice: x: 2, y: 2, z: 4, core: 2. Of those that a mesh axis runs over, the one named last changes fastest.
Arguments:
- prognostic_arrays: float32 [16, 3, 32, 2688], P(None, None, ('lat', 'lev')), may hold values from -6 to 6
- coriolis: float32 [32], P(('lat', 'lev')), may hold values from -1.5 to 1.5
- weights: float32 [32], P(('lat', 'lev')), may hold values from 0.5 to 2
- row_points: int32 [32], P(('lat', 'lev')), may hold values from 196 to 2688, as said below
- owner_pairs: int32 [8, 6], replicated, may hold values from 0 to 47, as said below
- legendre: bfloat16 [8, 6, 97, 32], P('lev', None, None, 'lat'), may hold values from -2 to 2
- depths: float32 [16], replicated, may hold values from 0.5 to 8
- diffusion: float32 [16], replicated, may hold values from 0.5 to 8
Outputs:
- updated: float32 [16, 3, 32, 2688], P(None, None, ('lat', 'lev'))
Inputs may be any that keep to these rules, and one draw needn't show every extreme that they name: `owner_pairs`: a permutation of the pair indices 0 .. 47, 6 to each owner; pair s stands for the wavenumbers s and 95 - s. `row_points`: multiples of 4; some row has exactly 2688 points and some exactly 196.
All inputs are finite; a program needn't handle non-finite values.
Results may differ from a plain program's by a relative error of at most 0.0058.
Values may be sent and summed in bfloat16 or wider, within the bound.
No kernel may reach another device: no remote copies, remote signals or barrier semaphores. Data moves between devices by JAX's collectives and lax.ppermute only.
A program may use at most 64 MiB of HBM per device.

v0:
```python
import math
import jax
import jax.numpy as jnp
from jax import lax
from jax.sharding import PartitionSpec as P

stepsize_delta = 0.5


def tendencies(prognostic_arrays, coriolis):
    vorticity = prognostic_arrays[:, 0]
    spreading_rate_grid = prognostic_arrays[:, 1]
    thermal_state_grid = prognostic_arrays[:, 2]
    rotation = coriolis[None, :, None]
    advanced_curl_rate = vorticity - stepsize_delta * (rotation + vorticity) * spreading_rate_grid
    advanced_spreading_rate = spreading_rate_grid + stepsize_delta * (
        rotation * vorticity - spreading_rate_grid * spreading_rate_grid
    )
    advanced_thermal_state = (
        thermal_state_grid - stepsize_delta * thermal_state_grid * spreading_rate_grid
    )
    return jnp.stack(
        [advanced_curl_rate, advanced_spreading_rate, advanced_thermal_state], axis=1
    ).astype(jnp.bfloat16)


def owner_waves(owner_pairs, highest):
    return jnp.stack([owner_pairs, highest - 1 - owner_pairs], axis=1)


def phase_table(points, wavenumbers, lon_count):
    positions = jnp.arange(lon_count, dtype=jnp.int32)
    product = positions[None, :, None] * wavenumbers[None, None, :] % points[:, None, None]
    angle = (
        product.astype(jnp.float32) * (2.0 * math.pi / points.astype(jnp.float32))[:, None, None]
    )
    return jnp.stack([jnp.cos(angle), -jnp.sin(angle)], axis=2).astype(jnp.bfloat16)


def valid_points(points, lon_count):
    positions = jnp.arange(lon_count, dtype=jnp.int32)
    return positions[None, :] < points[:, None]


def half_mask(my_pairs, slot_total):
    positions = jnp.arange(slot_total, dtype=jnp.int32)
    return positions[None, :] < (slot_total - 1 - my_pairs)[:, None]


def implicit(summed, my_pairs, depth_part, diff_part):
    slot_total = summed.shape[3]
    slot_count = summed.shape[2]
    highest = slot_total - 1
    positions = jnp.arange(slot_total, dtype=jnp.int32)[None, :]
    first_half = positions < (highest - my_pairs)[:, None]
    total = jnp.where(first_half, my_pairs[:, None] + positions, positions - 1).astype(jnp.float32)
    harmonic_operator_spectrum = total * (total + 1.0) / float(highest * highest)
    bundled_prognostics = summed.reshape(-1, 3, 2, slot_count, slot_total)
    vorticity = bundled_prognostics[:, 0]
    spreading_rate_grid = bundled_prognostics[:, 1]
    thermal_state_grid = bundled_prognostics[:, 2]
    layer_stack_count = depth_part[:, None, None, None]
    diff_cols = diff_part[:, None, None, None]
    advanced_curl_rate = vorticity / (
        1.0 + diff_cols * harmonic_operator_spectrum * harmonic_operator_spectrum
    )
    advanced_spreading_rate = (
        spreading_rate_grid + harmonic_operator_spectrum * thermal_state_grid
    ) / (1.0 + layer_stack_count * harmonic_operator_spectrum)
    advanced_thermal_state = thermal_state_grid - layer_stack_count * advanced_spreading_rate
    piled_prognostics = jnp.stack(
        [advanced_curl_rate, advanced_spreading_rate, advanced_thermal_state], axis=1
    )
    return piled_prognostics.reshape(summed.shape).astype(jnp.bfloat16)


def body(
    prognostic_arrays, coriolis, weights, row_points, owner_pairs, legendre, depths, diffusion
):
    levels = prognostic_arrays.shape[0]
    row_count = prognostic_arrays.shape[2]
    lon_count = prognostic_arrays.shape[3]
    group_count = owner_pairs.shape[0]
    slot_count = owner_pairs.shape[1]
    local_basis = legendre[0]
    slot_total = local_basis.shape[1]
    highest = slot_total - 1
    channels = levels * 3
    packed = channels * 4 * slot_count
    wavenumbers = owner_waves(owner_pairs, highest).reshape(-1)
    valid = valid_points(row_points, lon_count)
    gridded = tendencies(prognostic_arrays, coriolis).reshape(channels, row_count, lon_count)
    gridded = jnp.where(valid[None], gridded, jnp.zeros((), gridded.dtype))
    phases = phase_table(row_points, wavenumbers, lon_count).reshape(
        row_count, lon_count, 2, group_count, 2, slot_count
    )
    row_scale = weights / row_points.astype(jnp.float32)
    fourier = jnp.einsum("crx,rxqght->grcqht", gridded, phases, preferred_element_type=jnp.float32)
    fourier = (fourier * row_scale[None, :, None, None, None, None]).astype(jnp.bfloat16)
    band_data = lax.all_to_all(
        fourier.reshape(group_count, row_count, packed),
        "lev",
        split_axis=0,
        concat_axis=0,
        tiled=True,
    )
    band_block = band_data.reshape(group_count * row_count, channels, 2, 2, slot_count)
    owner_index = lax.axis_index("lev")
    my_pairs = lax.dynamic_index_in_dim(owner_pairs, owner_index, 0, keepdims=False)
    first_half = half_mask(my_pairs, slot_total)
    half_masks = jnp.stack([first_half, jnp.logical_not(first_half)], axis=0)
    doubling = jnp.where(owner_waves(my_pairs[None], highest)[0] == 0, 1.0, 2.0).astype(jnp.float32)
    both_halves = jnp.einsum(
        "lkqht,tpl->kqhtp", band_block, local_basis, preferred_element_type=jnp.float32
    )
    summed = lax.psum(jnp.where(first_half, both_halves[:, :, 0], both_halves[:, :, 1]), "lat")
    solved = implicit(summed, my_pairs, depths, diffusion)
    masked_spec = jnp.where(half_masks[None, None], solved[:, :, None], jnp.zeros((), solved.dtype))
    inverted = jnp.einsum(
        "kqhtp,tpl->lkqht", masked_spec, local_basis, preferred_element_type=jnp.float32
    )
    inverted = (inverted * doubling[None, None, None]).astype(jnp.bfloat16)
    returned = lax.all_to_all(
        inverted.reshape(group_count, row_count, packed),
        "lev",
        split_axis=0,
        concat_axis=0,
        tiled=True,
    )
    returned = returned.reshape(group_count, row_count, channels, 2, 2, slot_count)
    outgrid = jnp.einsum("grcqht,rxqght->crx", returned, phases, preferred_element_type=jnp.float32)
    outgrid = jnp.where(valid[None], outgrid, jnp.zeros((), outgrid.dtype))
    return outgrid.reshape(levels, 3, row_count, lon_count)


def solution(mesh):
    in_specs = (
        P(None, None, ("lat", "lev"), None),
        P(("lat", "lev")),
        P(("lat", "lev")),
        P(("lat", "lev")),
        P(),
        P("lev", None, None, "lat"),
        P(),
        P(),
    )
    out_specs = P(None, None, ("lat", "lev"), None)
    return jax.shard_map(body, mesh=mesh, in_specs=in_specs, out_specs=out_specs, check_vma=False)
```

profile of v0, /device:TPU:0, one launch (start us, length us, event | category | flops | bytes accessed | tf_op | source)
XLA Modules:
  0.0 103.7 jit_solution(4373034234354708365)
XLA Ops:
  7.2 0.7 copy-done.2
  8.6 1.8 %subtract_convert_fusion.1 = (bf16[16,1,1,2688]{3,2,1,0:T(2,128)(2,1)S(1)}, bf16[16,1,1,2688]{3,2,1,0:T(2,128)(2,1)S(1)}, bf16[16,1,1,2688]{3,2,1,0:T(2,128)(2,1)S(1)}) fusion(f32[16,3,1,2688]{3,2,1,0:T(1,128)} %param.8, f32[]{:T(128)} %bitcast.73), kind=kLoop, calls=%fused_computation.33 | loop fusion | flops 645120 | bytes 774148 | tf_op jit(solution)/shard_map/convert.3
  10.4 1.5 %maximum_reduce_fusion = bf16[16,3,2688]{2,1,0:T(4,128)(2,1)S(1)} fusion(bf16[16,1,1,2688]{3,2,1,0:T(2,128)(2,1)S(1)} %get-tuple-element.11, bf16[16,1,1,2688]{3,2,1,0:T(2,128)(2,1)S(1)} %get-tuple-element.10, bf16[16,1,1,2688]{3,2,1,0:T(2,128)(2,1)S(1)} %get-tuple-element.9), kind=kLoop, calls=%fused_computation.22 | loop fusion | flops 258048 | bytes 516096 | tf_op jit(solution)/shard_map/stack | solution.py:22
  11.9 0.2 convert_element_type.67
  12.9 14.4 %cosine_convert_fusion = (bf16[2688,1,8,2,6]{0,2,4,3,1:T(8,128)(2,1)S(1)}, bf16[2688,1,8,2,6]{0,2,4,3,1:T(8,128)(2,1)S(1)}) fusion(f32[]{:T(128)} %bitcast.6, s32[]{:T(128)} %bitcast.4, s32[8,2,6]{0,2,1:T(8,128)S(1)} %copy.24, pred[]{:T(512)} %bitcast.5), kind=kLoop, calls=%fused_computation.16 | loop fusion | flops 3354624 | bytes 1032585 | tf_op jit(solution)/shard_map/convert.6
  27.2 0.4 fusion.5
  27.7 0.7 copy.25
  28.3 0.6 reshape.376
  29.0 0.5 broadcast.353
  29.5 0.6 reduce.4
  30.1 0.7 reshape.381
  30.8 7.3 %all-to-all-start = ((bf16[8,2,576]{2,1,0:T(2,128)(2,1)}), bf16[8,2,576]{2,1,0:T(2,128)(2,1)S(1)}, u32[]{:S(2)}, u32[]{:S(2)}) async-start(bf16[8,2,576]{2,1,0:T(2,128)(2,1)} %reshape.381), calls=%async_computation | async-start | bytes 40960 | tf_op jit(solution)/shard_map/all_to_all | solution.py:100
  38.5 0.6 copy-done.3
  39.3 5.5 %all-to-all-done = bf16[8,2,576]{2,1,0:T(2,128)(2,1)S(1)} async-done(((bf16[8,2,576]{2,1,0:T(2,128)(2,1)}), bf16[8,2,576]{2,1,0:T(2,128)(2,1)S(1)}, u32[]{:S(2)}, u32[]{:S(2)}) %all-to-all-start) | async-done | bytes 18464 | tf_op jit(solution)/shard_map/all_to_all | solution.py:100
  44.8 0.1 reduce.1
  44.9 0.8 reshape.368
  45.8 0.7 copy.27
  46.5 0.3 convolution_bitcast_fusion.1
  46.8 0.9 copy.29
  47.7 29.9 %all-reduce.2.cloned.1.call-done = f32[16,3,2,6,97]{4,2,3,1,0:T(2,128)} async-done(((f32[16,3,2,6,97]{4,2,3,1,0:T(2,128)}), f32[16,3,2,6,97]{4,2,3,1,0:T(2,128)}) %all-reduce.2.cloned.1.call-update) | async-done | bytes 223504 | tf_op jit(solution)/shard_map/psum | solution.py:116
  77.6 1.1 %fusion.31 = (bf16[16,1,2,6,97]{4,2,3,1,0:T(2,128)(2,1)S(1)}, f32[16,1,2,6,97]{4,2,3,1,0:T(2,128)S(1)}) fusion(f32[16,6,97]{2,1,0:T(8,128)S(1)} %get-tuple-element.17, f32[16,3,2,6,97]{4,2,3,1,0:T(2,128)} %all-reduce.2.cloned.1.call-done, f32[6,97]{1,0:T(8,128)S(1)} %fusion.26), kind=kLoop, calls=%fused_computation.64 | loop fusion | flops 74496 | bytes 300312 | tf_op jit(solution)/shard_map/convert.1
  78.7 0.1 fusion.23
  78.9 0.2 pad_maximum_fusion.1
  79.1 0.4 fusion.4
  79.5 0.7 copy.32
  80.2 0.6 reshape.377
  80.8 0.6 reduce.5
  81.6 11.9 %all_to_all.10 = bf16[8,2,576]{2,1,0:T(2,128)(2,1)S(1)} all-to-all(bf16[8,2,576]{2,1,0:T(2,128)(2,1)S(1)} %reshape.383), channel_id=1, replica_groups=mesh['lat'=4,'lev'=8] {'lev'}, dimensions={0} | all-to-all | bytes 36864 | tf_op jit(solution)/shard_map/all_to_all | solution.py:123
  93.7 0.8 reshape.371
  94.5 0.7 copy.35
  95.2 0.4 fusion.1
  95.6 1.3 %reshape.372 = f32[16,3,1,2688]{3,2,1,0:T(1,128)} reshape(f32[48,1,2688]{2,0,1:T(8,128)S(1)} %fusion.1) | data formatting | bytes 1032192 | tf_op jit(solution)/shard_map/reshape | solution.py:133
  (30 shorter events, 1.1 us)
Async XLA Ops:
  6.5 39.9 %copy-start = (bf16[1,6,97,8]{2,3,1,0:T(8,128)(2,1)S(1)}, bf16[1,6,97,8]{2,3,1,0:T(8,128)(2,1)}, u32[]{:S(2)}) copy-start(bf16[1,6,97,8]{2,3,1,0:T(8,128)(2,1)} %param.13) | copy-start | bytes 27940
  7.2 0.7 copy-start.2
  30.8 13.9 %all-to-all-start = ((bf16[8,2,576]{2,1,0:T(2,128)(2,1)}), bf16[8,2,576]{2,1,0:T(2,128)(2,1)S(1)}, u32[]{:S(2)}, u32[]{:S(2)}) async-start(bf16[8,2,576]{2,1,0:T(2,128)(2,1)} %reshape.381), calls=%async_computation | async-start | bytes 40960 | tf_op jit(solution)/shard_map/all_to_all | solution.py:100
  38.1 39.5 %all-reduce.2.cloned.1.call-start = ((), (), s32[]{:S(2)}) async-start(), calls=%async_computation.2 | async-start | bytes 589824 | tf_op jit(solution)/shard_map/psum | solution.py:116
  38.4 0.7 copy-start.3
  38.4 0.7 copy-start.4
  77.6 1.1 %copy-start.1 = (f32[16,3,2,6,97]{4,2,3,1,0:T(2,128)S(1)}, f32[16,3,2,6,97]{4,2,3,1,0:T(2,128)}, u32[]{:S(2)}) copy-start(f32[16,3,2,6,97]{4,2,3,1,0:T(2,128)} %all-reduce.2.cloned.1.call-done) | copy-start | bytes 670468
Sparse Core Ops, SparseCore 0:
  47.8 29.7 all-reduce.1
where the time goes:
time: 104 us
  waiting for transfers between devices  35.4 us (34%)
  other arithmetic  21 us (20%)
  between operations  15.7 us (15%)
  blocking collectives  11.9 us (11%)
  local copies, waits for them, and re-layouts  10.9 us (10%)
  starting transfers between devices  7.35 us (7%)
  matrix products  1.47 us (1%)
    psum x1, waiting for transfers between devices, body(): lax.psum(jnp.where(first_half, both_halves[:, :, 0], both_halves[:, :, 1]...  29.9 us
    another operation x4, other arithmetic  17.4 us
    all_to_all x1, blocking collectives, body(): lax.all_to_all(inverted.reshape(group_count, row_count, packed), 'lev', s...  11.9 us
    all_to_all x1, starting transfers between devices, body(): lax.all_to_all(fourier.reshape(group_count, row_count, packed), 'lev', sp...  7.31 us
    all_to_all x1, waiting for transfers between devices, body(): lax.all_to_all(fourier.reshape(group_count, row_count, packed), 'lev', sp...  5.47 us
    unnamed x14, local copies, waits for them, and re-layouts  2.26 us
  transfers between devices with their start and end apart: 2, of which 2 were waited for; matrix products, arithmetic and copies ran while one was open for 0% of the time, Pallas kernels for 0%

commit v1 on v0

--- a/solution.py
+++ b/solution.py
@@ -113,7 +113,10 @@
     both_halves = jnp.einsum(
         "lkqht,tpl->kqhtp", band_block, local_basis, preferred_element_type=jnp.float32
     )
-    summed = lax.psum(jnp.where(first_half, both_halves[:, :, 0], both_halves[:, :, 1]), "lat")
+    summed = jnp.sum(
+        lax.all_gather(jnp.where(first_half, both_halves[:, :, 0], both_halves[:, :, 1]), "lat"),
+        axis=0,
+    )
     solved = implicit(summed, my_pairs, depths, diffusion)
     masked_spec = jnp.where(half_masks[None, None], solved[:, :, None], jnp.zeros((), solved.dtype))
     inverted = jnp.einsum(

time: 104 us -> 68.2 us (0.66)
  waiting for transfers between devices: 35.4 us -> 5.4 us
  between operations: 15.7 us -> 2.3 us
  blocking collectives: 11.9 us -> 19.7 us
  local copies, waits for them, and re-layouts: 10.9 us -> 9.19 us
  other arithmetic: 21 us -> 22.5 us
    psum x1 -> x0, waiting for transfers between devices: 29.9 us -> none  [body(): lax.psum(jnp.where(first_half, both_halves[:, :, 0], both_halves[:, :, 1]...]
    all_gather x0 -> x1, blocking collectives: none -> 10.7 us  [body(): lax.all_gather(jnp.where(first_half, both_halves[:, :, 0], both_halves[:,...]
    all_to_all x1, blocking collectives: 11.9 us -> 8.97 us  [body(): lax.all_to_all(inverted.reshape(group_count, row_count, packed), 'lev', s...]
    another operation x3, other arithmetic: 0.02 us -> 2.08 us  [owner_waves(): return jnp.stack([owner_pairs, highest - 1 - owner_pairs], axis=1)]
    unnamed x14 -> x10, local copies, waits for them, and re-layouts: 2.26 us -> 1.02 us
  transfers between devices with their start and end apart: 2 -> 1, of which waited for: 2 -> 1; matrix products, arithmetic and copies ran while one was open for 0% -> 2% of each run, Pallas kernels for 0% -> 0%
where the time goes in v1:
time: 68.2 us; the launch traced here: 67.8 us
  other arithmetic  22.5 us (33%)
  blocking collectives  19.7 us (29%)
  local copies, waits for them, and re-layouts  9.19 us (13%)
  starting transfers between devices  7.31 us (11%)
  waiting for transfers between devices  5.4 us (8%)
  between operations  2.3 us (3%)
  matrix products  1.46 us (2%)
    another operation x4, other arithmetic  16.4 us
    all_gather x1, blocking collectives, body(): lax.all_gather(jnp.where(first_half, both_halves[:, :, 0], both_halves[:,...  10.7 us
    all_to_all x1, blocking collectives, body(): lax.all_to_all(inverted.reshape(group_count, row_count, packed), 'lev', s...  8.97 us
    all_to_all x1, starting transfers between devices, body(): lax.all_to_all(fourier.reshape(group_count, row_count, packed), 'lev', sp...  7.31 us
    all_to_all x1, waiting for transfers between devices, body(): lax.all_to_all(fourier.reshape(group_count, row_count, packed), 'lev', sp...  5.4 us
    another operation x3, other arithmetic, owner_waves(): return jnp.stack([owner_pairs, highest - 1 - owner_pairs], axis=1)  2.08 us
    reshape x2, local copies, waits for them, and re-layouts, body(): band_data.reshape(group_count * row_count, channels, 2, 2, slot_count)  1.52 us
    another operation x2, local copies, waits for them, and re-layouts  1.51 us
  transfers between devices with their start and end apart: 1, of which 1 were waited for; matrix products, arithmetic and copies ran while one was open for 2% of the time, Pallas kernels for 0%

profile of v1, /device:TPU:0, one launch (start us, length us, event | category | flops | bytes accessed | tf_op | source)
XLA Modules:
  0.0 67.8 jit_solution(379380462245674463)
XLA Ops:
  0.7 0.7 %subtract_bitcast_fusion = s32[8,1,6]{2,0,1:T(8,128)S(1)} fusion(s32[8,6]{1,0:T(8,128)} %param.12), kind=kLoop, calls=%fused_computation.53 | loop fusion | flops 48 | bytes 384 | tf_op jit(solution)/shard_map/stack | solution.py:28
  1.4 0.7 %pad_add_fusion.1 = s32[8,2,6]{2,0,1:T(8,128)S(1)} fusion(s32[8,1,6]{2,0,1:T(8,128)S(1)} %subtract_bitcast_fusion, s32[8,1,6]{2,0,1:T(8,128)} %bitcast.80), kind=kLoop, calls=%fused_computation.49 | loop fusion | flops 96 | bytes 768 | tf_op jit(solution)/shard_map/stack | solution.py:28
  2.8 1.8 %subtract_convert_fusion.1 = (bf16[16,1,1,2688]{3,2,1,0:T(2,128)(2,1)S(1)}, bf16[16,1,1,2688]{3,2,1,0:T(2,128)(2,1)S(1)}, bf16[16,1,1,2688]{3,2,1,0:T(2,128)(2,1)S(1)}) fusion(f32[16,3,1,2688]{3,2,1,0:T(1,128)} %param.8, f32[]{:T(128)} %bitcast.73), kind=kLoop, calls=%fused_computation.33 | loop fusion | flops 645120 | bytes 774148 | tf_op jit(solution)/shard_map/convert.3
  4.6 1.5 %maximum_reduce_fusion = bf16[16,3,2688]{2,1,0:T(4,128)(2,1)S(1)} fusion(bf16[16,1,1,2688]{3,2,1,0:T(2,128)(2,1)S(1)} %get-tuple-element.11, bf16[16,1,1,2688]{3,2,1,0:T(2,128)(2,1)S(1)} %get-tuple-element.10, bf16[16,1,1,2688]{3,2,1,0:T(2,128)(2,1)S(1)} %get-tuple-element.9), kind=kLoop, calls=%fused_computation.22 | loop fusion | flops 258048 | bytes 516096 | tf_op jit(solution)/shard_map/stack | solution.py:22
  6.0 0.2 convert_element_type.67
  7.0 14.4 %cosine_convert_fusion = (bf16[2688,1,8,2,6]{0,2,4,3,1:T(8,128)(2,1)S(1)}, bf16[2688,1,8,2,6]{0,2,4,3,1:T(8,128)(2,1)S(1)}) fusion(f32[]{:T(128)} %bitcast.6, s32[]{:T(128)} %bitcast.4, s32[8,2,6]{0,2,1:T(8,128)S(1)} %copy.23, pred[]{:T(512)} %bitcast.5), kind=kLoop, calls=%fused_computation.16 | loop fusion | flops 3354624 | bytes 1032585 | tf_op jit(solution)/shard_map/convert.6
  21.4 0.4 fusion.5
  21.9 0.7 copy.24
  22.5 0.6 reshape.393
  23.2 0.6 broadcast.360
  23.7 0.8 %reduce.4 = bf16[8,1152]{1,0:T(8,128)(2,1)S(1)} reduce(bf16[8,1,1152]{2,1,0:T(2,128)(2,1)S(1)} %reshape.393, bf16[]{:T(256)} %broadcast.360), dimensions={1}, to_apply=%reshape.393.reduce_sub_computation | reduce | bytes 36866 | tf_op jit(solution)/shard_map/reshape | solution.py:101
  24.5 0.7 %reshape.398 = bf16[8,2,576]{2,1,0:T(2,128)(2,1)} reshape(bf16[8,1152]{1,0:T(8,128)(2,1)S(1)} %reduce.4) | data formatting | bytes 36864
  25.2 7.3 %all-to-all-start = ((bf16[8,2,576]{2,1,0:T(2,128)(2,1)}), bf16[8,2,576]{2,1,0:T(2,128)(2,1)S(1)}, u32[]{:S(2)}, u32[]{:S(2)}) async-start(bf16[8,2,576]{2,1,0:T(2,128)(2,1)} %reshape.398), calls=%async_computation | async-start | bytes 40960 | tf_op jit(solution)/shard_map/all_to_all | solution.py:100
  32.6 0.7 %subtract_bitcast_fusion.1 = (s32[1,1,6]{2,1,0:T(1,128)S(1)}, s32[1,6]{1,0:T(1,128)S(1)}) fusion(s32[8,6]{1,0:T(8,128)} %param.12, s32[]{:T(128)S(6)} %select_n.79), kind=kLoop, calls=%fused_computation.57 | loop fusion | flops 6 | bytes 76 | tf_op jit(solution)/shard_map/stack | solution.py:28
  33.8 5.4 %all-to-all-done = bf16[8,2,576]{2,1,0:T(2,128)(2,1)S(1)} async-done(((bf16[8,2,576]{2,1,0:T(2,128)(2,1)}), bf16[8,2,576]{2,1,0:T(2,128)(2,1)S(1)}, u32[]{:S(2)}, u32[]{:S(2)}) %all-to-all-start) | async-done | bytes 18464 | tf_op jit(solution)/shard_map/all_to_all | solution.py:100
  39.3 0.1 reduce.1
  39.4 0.8 %reshape.385 = bf16[8,48,2,2,6]{4,3,2,1,0:T(2,128)(2,1)S(1)} reshape(bf16[8,1152]{1,0:T(8,128)(2,1)S(1)} %reduce.1) | data formatting | bytes 36864 | tf_op jit(solution)/shard_map/reshape | solution.py:107
  40.2 0.7 %copy.26 = bf16[8,48,2,2,6]{1,0,3,2,4:T(8,128)(2,1)S(1)} copy(bf16[8,48,2,2,6]{4,3,2,1,0:T(2,128)(2,1)S(1)} %reshape.385) | data formatting | bytes 36864 | tf_op jit(solution)/shard_map/reshape | solution.py:107
  40.9 0.3 convolution_bitcast_fusion.1
  41.3 10.7 %all_gather.4 = f32[4,48,2,6,97]{4,1,3,2,0:T(8,128)S(1)} all-gather(f32[1,48,2,6,97]{4,1,3,2,0:T(8,128)S(1)} %copy.28), channel_id=1, replica_groups=mesh['lat'=4,'lev'=8] {'lat'}, dimensions={0}, use_global_device_ids=true | all-gather | bytes 1117440 | tf_op jit(solution)/shard_map/all_gather | solution.py:117
  52.1 0.2 copy.30
  52.5 0.1 fusion.23
  52.6 0.2 pad_maximum_fusion.1
  52.9 0.4 fusion.4
  53.3 0.7 copy.33
  53.9 0.6 reshape.394
  54.6 0.8 %reduce.5 = bf16[8,1152]{1,0:T(8,128)(2,1)S(1)} reduce(bf16[8,1,1152]{2,1,0:T(2,128)(2,1)S(1)} %reshape.394, bf16[]{:T(256)} %broadcast.360), dimensions={1}, to_apply=%reshape.394.reduce_sub_computation | reduce | bytes 36866 | tf_op jit(solution)/shard_map/reshape | solution.py:127
  55.5 9.0 %all_to_all.10 = bf16[8,2,576]{2,1,0:T(2,128)(2,1)S(1)} all-to-all(bf16[8,2,576]{2,1,0:T(2,128)(2,1)S(1)} %reshape.400), channel_id=1, replica_groups=mesh['lat'=4,'lev'=8] {'lev'}, dimensions={0} | all-to-all | bytes 36864 | tf_op jit(solution)/shard_map/all_to_all | solution.py:126
  64.7 0.8 %reshape.388 = bf16[8,48,2,2,6]{4,3,2,1,0:T(2,128)(2,1)S(1)} reshape(bf16[8,1152]{1,0:T(8,128)(2,1)S(1)} %reduce.2) | data formatting | bytes 36864 | tf_op jit(solution)/shard_map/reshape.33
  65.5 0.7 %copy.36 = bf16[8,48,2,2,6]{1,0,4,2,3:T(8,128)(2,1)S(1)} copy(bf16[8,48,2,2,6]{4,3,2,1,0:T(2,128)(2,1)S(1)} %reshape.388) | data formatting | bytes 36864 | tf_op jit(solution)/shard_map/reshape.33
  66.2 0.4 fusion.1
  66.5 1.3 %reshape.389 = f32[16,3,1,2688]{3,2,1,0:T(1,128)} reshape(f32[48,1,2688]{2,0,1:T(8,128)S(1)} %fusion.1) | data formatting | bytes 1032192 | tf_op jit(solution)/shard_map/reshape | solution.py:136
  (26 shorter events, 1.2 us)
Async XLA Ops:
  0.0 40.9 %copy-start = (bf16[1,6,97,8]{2,3,1,0:T(8,128)(2,1)S(1)}, bf16[1,6,97,8]{2,3,1,0:T(8,128)(2,1)}, u32[]{:S(2)}) copy-start(bf16[1,6,97,8]{2,3,1,0:T(8,128)(2,1)} %param.13) | copy-start | bytes 27940
  21.4 12.1 %copy-start.1 = (f32[16]{0:T(128)S(1)}, f32[16]{0:T(128)}, u32[]{:S(2)}) copy-start(f32[16]{0:T(128)} %param.14) | copy-start | bytes 196
  21.4 12.1 %copy-start.2 = (f32[16]{0:T(128)S(1)}, f32[16]{0:T(128)}, u32[]{:S(2)}) copy-start(f32[16]{0:T(128)} %param.15) | copy-start | bytes 196
  25.2 13.9 %all-to-all-start = ((bf16[8,2,576]{2,1,0:T(2,128)(2,1)}), bf16[8,2,576]{2,1,0:T(2,128)(2,1)S(1)}, u32[]{:S(2)}, u32[]{:S(2)}) async-start(bf16[8,2,576]{2,1,0:T(2,128)(2,1)} %reshape.398), calls=%async_computation | async-start | bytes 40960 | tf_op jit(solution)/shard_map/all_to_all | solution.py:100
